TPU v7x, 128 devices: a whole 4x4x4 slice. The times are simulated.
128 devices in a mesh: section: 2 (over core), blk: 16 (over y, x), mp: 4 (over z).
Axes of the slice: x: 4, y: 4, z: 4, core: 2. Of those that a mesh axis runs over, the one named last changes fastest.
Arguments:
- patches: bfloat16 [256, 5120], P('section'), may hold values from -6 to 6
- merge_gain: float32 [1280], replicated, may hold values from 0.25 to 1.75
- merge_first: bfloat16 [5120, 5120], P(None, ('blk', 'mp')), may hold values from -0.078125 to 0.078125
- merge_second: bfloat16 [5120, 4096], P(('blk', 'mp')), may hold values from -0.078125 to 0.078125
- text_embeds: bfloat16 [4, 1024, 4096], P(None, 'blk', 'mp'), may hold values from -7 to 14
- positions: int32 [256], replicated, may hold values from 0 to 4095, as said below
- segments: int32 [4096], replicated, may hold values from 0 to 2, never falling along the last dimension, each value on 1 to 2048 neighbouring positions
- norm_gain: float32 [2, 4096], P('section'), may hold values from 0.25 to 1.75
- query_weight: bfloat16 [2, 4096, 4096], P('section', 'blk', 'mp'), may hold values from -1 to 1
- keyval_weight: bfloat16 [2, 4096, 4, 2, 128], P('section', 'blk', 'mp'), may hold values from -1 to 1
- out_weight: bfloat16 [2, 4096, 4096], P('section', 'mp', 'blk'), may hold values from -0.09375 to 0.09375
Outputs:
- hidden: bfloat16 [2, 4, 1024, 4096], P('section', None, 'blk', 'mp')
Inputs may be any that keep to these rules, and one draw needn't show every extreme that they name: `positions`: distinct and increasing.
All inputs are finite; a program needn't handle non-finite values.
Results may differ from a plain program's by a relative error of at most 0.015.
Values may be sent and summed in bfloat16 or wider, within the bound.
No kernel may reach another device: no remote copies, remote signals or barrier semaphores. Data moves between devices by JAX's collectives and lax.ppermute only.
A program may use at most 128 MiB of HBM per device.

v0:
```python
import jax
import jax.numpy as jnp
from jax import lax
from jax.sharding import PartitionSpec as P

epsilon = 1e-06
rope_base = 1000000.0


def shifted(value, axis, by):
    size = lax.axis_size(axis)
    pairs = [(i, i + by) for i in range(size) if 0 <= i + by < size]
    return lax.ppermute(value, axis, pairs)


def rope_tables(where_at, head_size):
    steps_half = jnp.arange(head_size // 2).astype(jnp.float32)
    inverse = jnp.exp(-jnp.log(rope_base) * 2.0 * steps_half / head_size)
    angles = where_at.astype(jnp.float32)[:, None] * inverse[None, :]
    return (jnp.cos(angles), jnp.sin(angles))


def rotate(values, cosine, sine):
    half = values.shape[-1] // 2
    first = values[..., :half]
    second = values[..., half:]
    cosine = cosine[:, None, :]
    sine = sine[:, None, :]
    return jnp.concatenate(
        [first * cosine - second * sine, second * cosine + first * sine], axis=-1
    )


def local(
    patches,
    merge_gain,
    merge_first,
    merge_second,
    text_embeds,
    positions,
    segments,
    norm_gain,
    query_weight,
    keyval_weight,
    out_weight,
):
    count = patches.shape[0]
    width = merge_gain.shape[0]
    blocks = text_embeds.shape[0]
    rows_here = text_embeds.shape[1]
    slice_width = text_embeds.shape[2]
    seq_len = segments.shape[0]
    block_len = seq_len // blocks
    section_index = lax.axis_index("section")
    cycle_index = lax.axis_index("blk")
    model_index = lax.axis_index("mp")
    pieces = patches.astype(jnp.float32).reshape(count, -1, width)
    centered = pieces - jnp.mean(pieces, axis=-1, keepdims=True)
    variance = jnp.mean(centered * centered, axis=-1, keepdims=True)
    normed = (
        (centered * lax.rsqrt(variance + epsilon) * merge_gain)
        .reshape(count, -1)
        .astype(jnp.bfloat16)
    )
    inner = jax.nn.gelu(
        jnp.dot(normed, merge_first, preferred_element_type=jnp.float32), approximate=False
    ).astype(jnp.bfloat16)
    partial_merge = jnp.dot(inner, merge_second, preferred_element_type=jnp.float32)
    merged_full = lax.psum(partial_merge, ("blk", "mp")).astype(jnp.bfloat16)
    merged_mine = lax.dynamic_slice_in_dim(merged_full, model_index * slice_width, slice_width, 1)
    visual_all = lax.all_gather(merged_mine, "section", axis=0, tiled=True)
    query_full, keyval_full, out_full = (
        lax.all_gather(query_weight, "blk", axis=1, tiled=True),
        lax.all_gather(keyval_weight, "blk", axis=1, tiled=True),
        lax.all_gather(out_weight, "blk", axis=2, tiled=True),
    )
    query_full = query_full[0]
    kv_heads = keyval_full.shape[2]
    head_size = keyval_full.shape[4]
    keyval_full = keyval_full[0].reshape(keyval_full.shape[1], -1)
    out_full = out_full[0]
    gain_here = norm_gain[0]
    group = query_full.shape[1] // (kv_heads * head_size)
    scale = 1.0 / head_size**0.5
    key_where = jnp.arange(seq_len)
    ticks = blocks + lax.axis_size("section") - 1
    zero_index = jnp.zeros((), jnp.int32)
    held = jnp.zeros((rows_here, slice_width), jnp.bfloat16)
    cache_keys = jnp.zeros((seq_len, kv_heads, head_size), jnp.bfloat16)
    cache_values = jnp.zeros((seq_len, kv_heads, head_size), jnp.bfloat16)
    outputs = jnp.zeros((blocks, rows_here, slice_width), jnp.bfloat16)
    for tick_now in range(ticks):
        bound = min(tick_now + 1, blocks) * block_len
        block_now = tick_now - section_index
        active = (block_now >= 0) & (block_now < blocks)
        block_safe = jnp.clip(block_now, 0, blocks - 1)
        row_where = block_safe * block_len + cycle_index * rows_here + jnp.arange(rows_here)
        is_visual = positions[None, :] == row_where[:, None]
        picked = jnp.dot(
            is_visual.astype(jnp.bfloat16), visual_all, preferred_element_type=jnp.float32
        ).astype(jnp.bfloat16)
        text_rows = lax.dynamic_index_in_dim(text_embeds, block_safe, 0, keepdims=False)
        embedded = jnp.where(jnp.any(is_visual, axis=1)[:, None], picked, text_rows)
        incoming = jnp.where(section_index == 0, embedded, held)
        features = lax.all_gather(incoming, "mp", axis=1, tiled=True)
        feat_f = features.astype(jnp.float32)
        normx = (
            feat_f
            * lax.rsqrt(jnp.mean(feat_f * feat_f, axis=-1, keepdims=True) + epsilon)
            * gain_here
        ).astype(jnp.bfloat16)
        cosine, sine = rope_tables(row_where, head_size)
        query = jnp.dot(normx, query_full, preferred_element_type=jnp.float32).reshape(
            rows_here, -1, head_size
        )
        query = (
            rotate(query, cosine, sine)
            .astype(jnp.bfloat16)
            .reshape(rows_here, kv_heads, group, head_size)
        )
        keyval = jnp.dot(normx, keyval_full, preferred_element_type=jnp.float32).reshape(
            rows_here, kv_heads, 2, head_size
        )
        new_keys = rotate(keyval[:, :, 0, :], cosine, sine).astype(jnp.bfloat16)
        new_values = keyval[:, :, 1, :].astype(jnp.bfloat16)
        block_keys, block_values = (
            lax.all_gather(new_keys, "blk", axis=0, tiled=True),
            lax.all_gather(new_values, "blk", axis=0, tiled=True),
        )
        start = block_safe * block_len
        cache_keys = jnp.where(
            active,
            lax.dynamic_update_slice(cache_keys, block_keys, (start, zero_index, zero_index)),
            cache_keys,
        )
        cache_values = jnp.where(
            active,
            lax.dynamic_update_slice(cache_values, block_values, (start, zero_index, zero_index)),
            cache_values,
        )
        keys_seen = cache_keys[:bound]
        values_seen = cache_values[:bound]
        scores = (
            jnp.einsum("qkgd,skd->kgqs", query, keys_seen, preferred_element_type=jnp.float32)
            * scale
        )
        row_segments = jnp.take(segments, row_where)
        allowed = (key_where[None, :bound] <= row_where[:, None]) & (
            segments[None, :bound] == row_segments[:, None]
        )
        scores = jnp.where(allowed[None, None], scores, -jnp.inf)
        top = jnp.max(scores, axis=-1, keepdims=True)
        expo = jnp.exp(scores - top)
        probs = (expo / jnp.sum(expo, axis=-1, keepdims=True)).astype(jnp.bfloat16)
        attended = jnp.einsum(
            "kgqs,skd->qkgd", probs, values_seen, preferred_element_type=jnp.float32
        )
        attended = attended.reshape(rows_here, -1).astype(jnp.bfloat16)
        term = jnp.dot(attended, out_full, preferred_element_type=jnp.float32)
        summed = lax.psum_scatter(
            term.astype(jnp.bfloat16), "mp", scatter_dimension=1, tiled=True
        ).astype(jnp.float32)
        result = (incoming.astype(jnp.float32) + summed).astype(jnp.bfloat16)
        outputs = jnp.where(
            active,
            lax.dynamic_update_slice(outputs, result[None], (block_safe, zero_index, zero_index)),
            outputs,
        )
        held = shifted(result, "section", 1)
    return outputs[None]


def solution(mesh):
    return jax.shard_map(
        local,
        mesh=mesh,
        in_specs=(
            P("section", None),
            P(),
            P(None, ("blk", "mp")),
            P(("blk", "mp"), None),
            P(None, "blk", "mp"),
            P(),
            P(),
            P("section", None),
            P("section", "blk", "mp"),
            P("section", "blk", "mp", None, None),
            P("section", "mp", "blk"),
        ),
        out_specs=P("section", None, "blk", "mp"),
        check_vma=False,
    )
```

profile of v0, /device:TPU:0, one launch (start us, length us, event | category | flops | bytes accessed | tf_op | source)
XLA Modules:
  0.0 948.9 jit_solution(6913599249277682439)
XLA Ops:
  8.8 2.9 reshape.1266
  16.2 5.2 fusion.210
  23.5 383.3 %all-reduce.1 = bf16[128,4096]{1,0:T(8,128)(2,1)S(1)} all-reduce(f32[128,4096]{1,0:T(8,128)} %fusion.210), channel_id=1, replica_groups=mesh['section'=2,'blk'=16,'mp'=4] {'blk','mp'}, use_global_device_ids=true, to_apply=%region_3.4 | all-reduce | flops 524288 | bytes 3145728 | tf_op jit(solution)/shard_map/psum | solution.py:69
  411.0 13.4 %all_gather.58 = bf16[64,4096]{1,0:T(8,128)(2,1)S(1)} all-gather(bf16[64,1024]{1,0:T(8,128)(2,1)S(1)} %fusion.63), channel_id=1, replica_groups=mesh['section'=2,'blk'=16,'mp'=4] {'mp'}, dimensions={1}, use_global_device_ids=true | all-gather | bytes 655360 | tf_op jit(solution)/shard_map/all_gather | solution.py:105
  426.1 4.7 copy.37
  432.0 20.7 %all_gather.61 = bf16[1024,1,128]{2,0,1:T(8,128)(2,1)S(1)} all-gather(bf16[64,1,128]{2,0,1:T(8,128)(2,1)S(1)} %pad_maximum_fusion), channel_id=1, replica_groups=mesh['section'=2,'blk'=16,'mp'=4] {'blk'}, dimensions={0}, use_global_device_ids=true | all-gather | bytes 278528 | tf_op jit(solution)/shard_map/all_gather | solution.py:127
  452.7 24.1 %all-gather = bf16[1024,1,1,128]{3,0,2,1:T(8,128)(2,1)S(1)} all-gather(bf16[64,1,1,128]{3,0,2,1:T(8,128)(2,1)S(1)} %slice.285), channel_id=2, replica_groups=mesh['section'=2,'blk'=16,'mp'=4] {'blk'}, dimensions={0}, use_global_device_ids=true | all-gather | bytes 278528 | tf_op jit(solution)/shard_map/all_gather | solution.py:128
  480.5 11.8 %copy.31 = bf16[1024,4096]{1,0:T(8,128)(2,1)} copy(bf16[1024,4096]{0,1:T(8,128)(2,1)} %bitcast.333) | data formatting | bytes 16777216 | tf_op jit(solution)/shard_map/dot_general | solution.py:113
  492.3 6.1 fusion.125
  502.2 5.8 fusion.13
  511.2 15.4 %reduce-scatter.6.cloned.1.call-done = bf16[64,1024]{1,0:T(8,128)(2,1)} async-done(((bf16[64,4096]{1,0:T(8,128)(2,1)}), bf16[64,1024]{1,0:T(8,128)(2,1)}) %reduce-scatter.6.cloned.1.call-update) | async-done | bytes 131088 | tf_op jit(solution)/shard_map/reduce_scatter | solution.py:160
  531.9 13.5 %all_gather.64 = bf16[64,4096]{1,0:T(8,128)(2,1)S(1)} all-gather(bf16[64,1024]{1,0:T(8,128)(2,1)S(1)} %fusion.65), channel_id=1, replica_groups=mesh['section'=2,'blk'=16,'mp'=4] {'mp'}, dimensions={1}, use_global_device_ids=true | all-gather | bytes 655360 | tf_op jit(solution)/shard_map/all_gather | solution.py:105
  546.5 6.1 fusion.128
  552.6 23.8 %all-gather.1 = bf16[1024,1,1,128]{3,0,2,1:T(8,128)(2,1)S(1)} all-gather(bf16[64,1,1,128]{3,0,2,1:T(8,128)(2,1)S(1)} %slice.284), channel_id=3, replica_groups=mesh['section'=2,'blk'=16,'mp'=4] {'blk'}, dimensions={0}, use_global_device_ids=true | all-gather | bytes 278528 | tf_op jit(solution)/shard_map/all_gather | solution.py:128
  576.7 23.3 %all_gather.66 = bf16[1024,1,128]{2,0,1:T(8,128)(2,1)S(1)} all-gather(bf16[64,1,128]{2,0,1:T(8,128)(2,1)S(1)} %pad_maximum_fusion.1), channel_id=1, replica_groups=mesh['section'=2,'blk'=16,'mp'=4] {'blk'}, dimensions={0}, use_global_device_ids=true | all-gather | bytes 278528 | tf_op jit(solution)/shard_map/all_gather | solution.py:127
  616.2 14.5 %reduce-scatter.8.cloned.1.call-done = bf16[64,1024]{1,0:T(8,128)(2,1)} async-done(((bf16[64,4096]{1,0:T(8,128)(2,1)}), bf16[64,1024]{1,0:T(8,128)(2,1)}) %reduce-scatter.8.cloned.1.call-update) | async-done | bytes 131088 | tf_op jit(solution)/shard_map/reduce_scatter | solution.py:160
  633.9 13.5 %all_gather.67 = bf16[64,4096]{1,0:T(8,128)(2,1)S(1)} all-gather(bf16[64,1024]{1,0:T(8,128)(2,1)S(1)} %broadcast_select_fusion.2), channel_id=1, replica_groups=mesh['section'=2,'blk'=16,'mp'=4] {'mp'}, dimensions={1}, use_global_device_ids=true | all-gather | bytes 655360 | tf_op jit(solution)/shard_map/all_gather | solution.py:105
  648.5 6.1 fusion.131
  654.6 23.8 %all-gather.2 = bf16[1024,1,1,128]{3,0,2,1:T(8,128)(2,1)S(1)} all-gather(bf16[64,1,1,128]{3,0,2,1:T(8,128)(2,1)S(1)} %slice.283), channel_id=4, replica_groups=mesh['section'=2,'blk'=16,'mp'=4] {'blk'}, dimensions={0}, use_global_device_ids=true | all-gather | bytes 278528 | tf_op jit(solution)/shard_map/all_gather | solution.py:128
  678.7 23.4 %all_gather.69 = bf16[1024,1,128]{2,0,1:T(8,128)(2,1)S(1)} all-gather(bf16[64,1,128]{2,0,1:T(8,128)(2,1)S(1)} %pad_maximum_fusion.2), channel_id=1, replica_groups=mesh['section'=2,'blk'=16,'mp'=4] {'blk'}, dimensions={0}, use_global_device_ids=true | all-gather | bytes 278528 | tf_op jit(solution)/shard_map/all_gather | solution.py:127
  715.8 17.7 %reduce-scatter.10.cloned.1.call-done = bf16[64,1024]{1,0:T(8,128)(2,1)} async-done(((bf16[64,4096]{1,0:T(8,128)(2,1)}), bf16[64,1024]{1,0:T(8,128)(2,1)}) %reduce-scatter.10.cloned.1.call-update) | async-done | bytes 131088 | tf_op jit(solution)/shard_map/reduce_scatter | solution.py:160
  737.7 13.4 %all_gather.70 = bf16[64,4096]{1,0:T(8,128)(2,1)S(1)} all-gather(bf16[64,1024]{1,0:T(8,128)(2,1)S(1)} %broadcast_select_fusion.1), channel_id=1, replica_groups=mesh['section'=2,'blk'=16,'mp'=4] {'mp'}, dimensions={1}, use_global_device_ids=true | all-gather | bytes 655360 | tf_op jit(solution)/shard_map/all_gather | solution.py:105
  752.1 6.1 fusion.134
  758.2 23.8 %all-gather.3 = bf16[1024,1,1,128]{3,0,2,1:T(8,128)(2,1)S(1)} all-gather(bf16[64,1,1,128]{3,0,2,1:T(8,128)(2,1)S(1)} %slice.282), channel_id=5, replica_groups=mesh['section'=2,'blk'=16,'mp'=4] {'blk'}, dimensions={0}, use_global_device_ids=true | all-gather | bytes 278528 | tf_op jit(solution)/shard_map/all_gather | solution.py:128
  782.3 23.2 %all_gather.72 = bf16[1024,1,128]{2,0,1:T(8,128)(2,1)S(1)} all-gather(bf16[64,1,128]{2,0,1:T(8,128)(2,1)S(1)} %pad_maximum_fusion.3), channel_id=1, replica_groups=mesh['section'=2,'blk'=16,'mp'=4] {'blk'}, dimensions={0}, use_global_device_ids=true | all-gather | bytes 278528 | tf_op jit(solution)/shard_map/all_gather | solution.py:127
  809.1 2.9 fusion.314
  818.7 18.8 %reduce-scatter.12.cloned.1.call-done = bf16[64,1024]{1,0:T(8,128)(2,1)} async-done(((bf16[64,4096]{1,0:T(8,128)(2,1)}), bf16[64,1024]{1,0:T(8,128)(2,1)}) %reduce-scatter.12.cloned.1.call-update) | async-done | bytes 131088 | tf_op jit(solution)/shard_map/reduce_scatter | solution.py:160
  844.1 12.8 %all_gather.73 = bf16[64,4096]{1,0:T(8,128)(2,1)S(1)} all-gather(bf16[64,1024]{1,0:T(8,128)(2,1)S(1)} %broadcast_select_fusion), channel_id=1, replica_groups=mesh['section'=2,'blk'=16,'mp'=4] {'mp'}, dimensions={1}, use_global_device_ids=true | all-gather | bytes 655360 | tf_op jit(solution)/shard_map/all_gather | solution.py:105
  857.9 6.1 fusion.137
  864.0 23.8 %all-gather.4 = bf16[1024,1,1,128]{3,0,2,1:T(8,128)(2,1)S(1)} all-gather(bf16[64,1,1,128]{3,0,2,1:T(8,128)(2,1)S(1)} %slice.281), channel_id=6, replica_groups=mesh['section'=2,'blk'=16,'mp'=4] {'blk'}, dimensions={0}, use_global_device_ids=true | all-gather | bytes 278528 | tf_op jit(solution)/shard_map/all_gather | solution.py:128
  888.0 23.3 %all_gather.75 = bf16[1024,1,128]{2,0,1:T(8,128)(2,1)S(1)} all-gather(bf16[64,1,128]{2,0,1:T(8,128)(2,1)S(1)} %pad_maximum_fusion.4), channel_id=1, replica_groups=mesh['section'=2,'blk'=16,'mp'=4] {'blk'}, dimensions={0}, use_global_device_ids=true | all-gather | bytes 278528 | tf_op jit(solution)/shard_map/all_gather | solution.py:127
  922.1 18.1 %reduce-scatter.14.cloned.1.call-done = bf16[64,1024]{1,0:T(8,128)(2,1)} async-done(((bf16[64,4096]{1,0:T(8,128)(2,1)}), bf16[64,1024]{1,0:T(8,128)(2,1)}) %reduce-scatter.14.cloned.1.call-update) | async-done | bytes 131088 | tf_op jit(solution)/shard_map/reduce_scatter | solution.py:160
  (308 shorter events, 102.9 us)
Async XLA Ops:
  6.5 419.6 %all-gather.9.cloned.1.call-start = ((), (), s32[]{:S(2)}) async-start(), calls=%async_computation.5 | async-start | bytes 2228224 | tf_op jit(solution)/shard_map/all_gather | solution.py:74
  7.3 473.2 %all-gather.11.cloned.1.call-start = ((), (), s32[]{:S(2)}) async-start(), calls=%async_computation.6 | async-start | bytes 8912896 | tf_op jit(solution)/shard_map/all_gather | solution.py:73
  8.0 494.1 %all-gather.13.cloned.1.call-start = ((), (), s32[]{:S(2)}) async-start(), calls=%async_computation.7 | async-start | bytes 8912896 | tf_op jit(solution)/shard_map/all_gather | solution.py:75
  8.7 517.9 %reduce-scatter.6.cloned.1.call-start = ((), (), s32[]{:S(2)}) async-start(), calls=%async_computation.8 | async-start | bytes 655360 | tf_op jit(solution)/shard_map/reduce_scatter | solution.py:160
  21.4 385.4 %copy-start.25 = (s32[256]{0:T(256)S(1)}, s32[256]{0:T(256)}, u32[]{:S(2)}) copy-start(s32[256]{0:T(256)} %param.18) | copy-start | bytes 3076
  21.4 403.2 %slice-start.8 = ((s32[4096]{0:T(1024)}), s32[1024]{0:T(1024)S(1)}, s32[]{:S(2)}) async-start(s32[4096]{0:T(1024)} %param.19), calls=%async_computation.21 | async-start | bytes 8192 | tf_op jit(solution)/shard_map/slice | solution.py:149
  21.4 404.6 %copy-start.46 = (f32[64]{0:T(128)}, f32[64]{0:T(128)S(1)}, u32[]{:S(2)}) copy-start(f32[64]{0:T(128)S(1)} %get-tuple-element.74) | copy-start | bytes 772
  22.2 554.2 %copy-start.26 = (f32[64]{0:T(128)}, f32[64]{0:T(128)S(1)}, u32[]{:S(2)}) copy-start(f32[64]{0:T(128)S(1)} %multiply_exponential_fusion) | copy-start | bytes 772
  22.2 384.6 %copy-start.44 = (s32[64]{0:T(128)}, s32[64]{0:T(128)S(1)}, u32[]{:S(2)}) copy-start(s32[64]{0:T(128)S(1)} %iota_add_fusion.5) | copy-start | bytes 772
  22.3 384.5 %copy-start.29 = (s32[64]{0:T(128)}, s32[64]{0:T(128)S(1)}, u32[]{:S(2)}) copy-start(s32[64]{0:T(128)S(1)} %get-tuple-element.77) | copy-start | bytes 772
  22.3 403.8 %copy-start.40 = (f32[64]{0:T(128)}, f32[64]{0:T(128)S(1)}, u32[]{:S(2)}) copy-start(f32[64]{0:T(128)S(1)} %get-tuple-element.80) | copy-start | bytes 772
  22.3 403.8 %copy-start.42 = (f32[64]{0:T(128)}, f32[64]{0:T(128)S(1)}, u32[]{:S(2)}) copy-start(f32[64]{0:T(128)S(1)} %get-tuple-element.79) | copy-start | bytes 772
  22.3 384.5 %copy-start.32 = (s32[64]{0:T(128)}, s32[64]{0:T(128)S(1)}, u32[]{:S(2)}) copy-start(s32[64]{0:T(128)S(1)} %get-tuple-element.75) | copy-start | bytes 772
  22.3 384.5 %copy-start.34 = (s32[64]{0:T(128)}, s32[64]{0:T(128)S(1)}, u32[]{:S(2)}) copy-start(s32[64]{0:T(128)S(1)} %get-tuple-element.76) | copy-start | bytes 772
  22.3 403.7 %copy-start.36 = (f32[64]{0:T(128)}, f32[64]{0:T(128)S(1)}, u32[]{:S(2)}) copy-start(f32[64]{0:T(128)S(1)} %get-tuple-element.82) | copy-start | bytes 772
  22.4 403.7 %copy-start.38 = (f32[64]{0:T(128)}, f32[64]{0:T(128)S(1)}, u32[]{:S(2)}) copy-start(f32[64]{0:T(128)S(1)} %get-tuple-element.81) | copy-start | bytes 772
  508.0 122.6 %reduce-scatter.8.cloned.1.call-start = ((), (), s32[]{:S(2)}) async-start(), calls=%async_computation.9 | async-start | bytes 655360 | tf_op jit(solution)/shard_map/reduce_scatter | solution.py:160
  527.7 2.4 collective-permute-start
  546.5 56.9 %copy-start.21 = (f32[64,64]{1,0:T(8,128)S(1)}, f32[64,64]{1,0:T(8,128)}, u32[]{:S(2)}) copy-start(f32[64,64]{1,0:T(8,128)} %get-tuple-element.51) | copy-start | bytes 49156
  546.5 56.9 %copy-start.22 = (f32[64,64]{1,0:T(8,128)S(1)}, f32[64,64]{1,0:T(8,128)}, u32[]{:S(2)}) copy-start(f32[64,64]{1,0:T(8,128)} %get-tuple-element.52) | copy-start | bytes 49156
  546.5 57.1 %copy-start.14 = (pred[64,2048]{1,0:T(8,128)(4,1)S(1)}, pred[64,2048]{1,0:T(8,128)(4,1)}, u32[]{:S(2)}) copy-start(pred[64,2048]{1,0:T(8,128)(4,1)} %compare_and_fusion.1) | copy-start | bytes 393220
  611.8 121.7 %reduce-scatter.10.cloned.1.call-start = ((), (), s32[]{:S(2)}) async-start(), calls=%async_computation.10 | async-start | bytes 655360 | tf_op jit(solution)/shard_map/reduce_scatter | solution.py:160
  631.6 2.3 collective-permute-start.1
  648.5 57.1 %copy-start.19 = (f32[64,64]{1,0:T(8,128)S(1)}, f32[64,64]{1,0:T(8,128)}, u32[]{:S(2)}) copy-start(f32[64,64]{1,0:T(8,128)} %get-tuple-element.53) | copy-start | bytes 49156
  648.5 57.1 %copy-start.20 = (f32[64,64]{1,0:T(8,128)S(1)}, f32[64,64]{1,0:T(8,128)}, u32[]{:S(2)}) copy-start(f32[64,64]{1,0:T(8,128)} %get-tuple-element.54) | copy-start | bytes 49156
  648.5 57.2 %copy-start.13 = (pred[64,3072]{1,0:T(8,128)(4,1)S(1)}, pred[64,3072]{1,0:T(8,128)(4,1)}, u32[]{:S(2)}) copy-start(pred[64,3072]{1,0:T(8,128)(4,1)} %compare_and_fusion) | copy-start | bytes 589828
  714.5 122.9 %reduce-scatter.12.cloned.1.call-start = ((), (), s32[]{:S(2)}) async-start(), calls=%async_computation.11 | async-start | bytes 655360 | tf_op jit(solution)/shard_map/reduce_scatter | solution.py:160
  734.5 2.5 collective-permute-start.2
  752.1 56.9 %copy-start.17 = (f32[64,64]{1,0:T(8,128)S(1)}, f32[64,64]{1,0:T(8,128)}, u32[]{:S(2)}) copy-start(f32[64,64]{1,0:T(8,128)} %get-tuple-element.55) | copy-start | bytes 49156
  752.1 57.0 %copy-start.3 = (pred[64,4096]{1,0:T(8,128)(4,1)S(1)}, pred[64,4096]{1,0:T(8,128)(4,1)}, u32[]{:S(2)}) copy-start(pred[64,4096]{1,0:T(8,128)(4,1)} %get-tuple-element.40) | copy-start | bytes 786436
  818.6 121.5 %reduce-scatter.14.cloned.1.call-start = ((), (), s32[]{:S(2)}) async-start(), calls=%async_computation.12 | async-start | bytes 655360 | tf_op jit(solution)/shard_map/reduce_scatter | solution.py:160
  838.5 4.9 collective-permute-start.3
  (50 other events, 668.7 us)
Sparse Core Ops, SparseCore 0:
  9.5 47.7 all-gather.8
  59.5 74.0 all-gather.10
  135.7 81.8 all-gather.12
  508.1 18.4 reduce-scatter.5
  611.9 18.7 reduce-scatter.7
  714.6 18.8 reduce-scatter.9
  818.8 18.6 reduce-scatter.11
  921.4 18.7 reduce-scatter.13
where the time goes:
time: 957 us; the launch traced here: 949 us
  blocking collectives  685 us (72%)
  waiting for transfers between devices  87 us (9%)
  matrix products  81.5 us (9%)
  other arithmetic  37.5 us (4%)
  local copies, waits for them, and re-layouts  37.3 us (4%)
  between operations  15.1 us (2%)
    psum x1, blocking collectives, local(): merged_full = lax.psum(partial_merge, ('blk', 'mp')).astype(jnp.bfloat16)  383 us
    all_gather x5, blocking collectives, local(): lax.all_gather(new_values, 'blk', axis=0, tiled=True)  119 us
    all_gather x5, blocking collectives, local(): lax.all_gather(new_keys, 'blk', axis=0, tiled=True)  114 us
    reduce_scatter x5, waiting for transfers between devices, local(): lax.psum_scatter(term.astype(jnp.bfloat16), 'mp', scatter_dimension=1, ti...  84.4 us
    all_gather x5, blocking collectives, local(): features = lax.all_gather(incoming, 'mp', axis=1, tiled=True)  66.5 us
    dot_general x5, matrix products, local(): jnp.dot(normx, query_full, preferred_element_type=jnp.float32)  30.4 us
  transfers between devices with their start and end apart: 12, of which 6 were waited for; matrix products, arithmetic and copies ran while one was open for 7% of the time, Pallas kernels for 0%

commit v1 on v0

--- a/solution.py
+++ b/solution.py
@@ -125,7 +125,9 @@
         new_values = keyval[:, :, 1, :].astype(jnp.bfloat16)
         block_keys, block_values = (
             lax.all_gather(new_keys, "blk", axis=0, tiled=True),
-            lax.all_gather(new_values, "blk", axis=0, tiled=True),
+            jnp.concatenate(
+                lax.all_to_all(jnp.stack([new_values] * lax.axis_size("blk")), "blk", 0, 0), axis=0
+            ),
         )
         start = block_safe * block_len
         cache_keys = jnp.where(

time: 957 us -> 919 us (0.960)
  blocking collectives: 685 us -> 574 us
  starting transfers between devices: 5.47 us -> 37.1 us
  matrix products: 81.5 us -> 101 us
  local copies, waits for them, and re-layouts: 37.3 us -> 53.2 us
    all_gather x5 -> x0, blocking collectives: 119 us -> none  [local(): lax.all_gather(new_values, 'blk', axis=0, tiled=True)]
    all_to_all x0 -> x5, starting transfers between devices: none -> 31.6 us  [local(): lax.all_to_all(jnp.stack([new_values] * lax.axis_size('blk')), 'blk', 0, 0)]
    unnamed x139 -> x127, local copies, waits for them, and re-layouts: 9.62 us -> 21.4 us
    dot_general x5, matrix products: 15.2 us -> 25.5 us  [local(): term = jnp.dot(attended, out_full, preferred_element_type=jnp.float32)]
  transfers between devices with their start and end apart: 12 -> 17, of which waited for: 6 -> 6; matrix products, arithmetic and copies ran while one was open for 7% -> 10% of each run, Pallas kernels for 0% -> 0%
where the time goes in v1:
time: 919 us; the launch traced here: 911 us
  blocking collectives  574 us (62%)
  matrix products  101 us (11%)
  waiting for transfers between devices  90.7 us (10%)
  local copies, waits for them, and re-layouts  53.2 us (6%)
  other arithmetic  40.6 us (4%)
  starting transfers between devices  37.1 us (4%)
  between operations  15.1 us (2%)
    psum x1, blocking collectives, local(): merged_full = lax.psum(partial_merge, ('blk', 'mp')).astype(jnp.bfloat16)  383 us
    all_gather x5, blocking collectives, local(): lax.all_gather(new_keys, 'blk', axis=0, tiled=True)  121 us
    reduce_scatter x5, waiting for transfers between devices, local(): lax.psum_scatter(term.astype(jnp.bfloat16), 'mp', scatter_dimension=1, ti...  88 us
    all_gather x5, blocking collectives, local(): features = lax.all_gather(incoming, 'mp', axis=1, tiled=True)  66.5 us
    all_to_all x5, starting transfers between devices, local(): lax.all_to_all(jnp.stack([new_values] * lax.axis_size('blk')), 'blk', 0, 0)  31.6 us
    dot_general x5, matrix products, local(): jnp.dot(normx, query_full, preferred_element_type=jnp.float32)  31.1 us
    dot_general x5, matrix products, local(): term = jnp.dot(attended, out_full, preferred_element_type=jnp.float32)  25.5 us
    unnamed x127, local copies, waits for them, and re-layouts  21.4 us
  transfers between devices with their start and end apart: 17, of which 6 were waited for; matrix products, arithmetic and copies ran while one was open for 10% of the time, Pallas kernels for 0%

profile of v1, /device:TPU:0, one launch (start us, length us, event | category | flops | bytes accessed | tf_op | source)
XLA Modules:
  0.0 910.8 jit_solution(10592025570657899442)
XLA Ops:
  16.2 5.2 fusion.207
  23.5 383.5 %all-reduce.1 = bf16[128,4096]{1,0:T(8,128)(2,1)S(1)} all-reduce(f32[128,4096]{1,0:T(8,128)} %fusion.207), channel_id=1, replica_groups=mesh['section'=2,'blk'=16,'mp'=4] {'blk','mp'}, use_global_device_ids=true, to_apply=%region_3.4 | all-reduce | flops 524288 | bytes 3145728 | tf_op jit(solution)/shard_map/psum | solution.py:69
  411.2 13.4 %all_gather.43 = bf16[64,4096]{1,0:T(8,128)(2,1)S(1)} all-gather(bf16[64,1024]{1,0:T(8,128)(2,1)S(1)} %fusion.63), channel_id=1, replica_groups=mesh['section'=2,'blk'=16,'mp'=4] {'mp'}, dimensions={1}, use_global_device_ids=true | all-gather | bytes 655360 | tf_op jit(solution)/shard_map/all_gather | solution.py:105
  437.2 24.2 %all_gather.45 = bf16[1024,1,128]{2,0,1:T(8,128)(2,1)S(1)} all-gather(bf16[64,1,128]{2,0,1:T(8,128)(2,1)S(1)} %pad_maximum_fusion), channel_id=1, replica_groups=mesh['section'=2,'blk'=16,'mp'=4] {'blk'}, dimensions={0}, use_global_device_ids=true | all-gather | bytes 278528 | tf_op jit(solution)/shard_map/all_gather | solution.py:127
  466.1 11.3 %copy.31 = bf16[1024,4096]{1,0:T(8,128)(2,1)} copy(bf16[1024,4096]{0,1:T(8,128)(2,1)} %bitcast.324) | data formatting | bytes 16777216 | tf_op jit(solution)/shard_map/dot_general | solution.py:113
  477.4 6.1 fusion.125
  487.4 5.8 fusion.13
  496.3 16.4 %reduce-scatter.6.cloned.1.call-done = bf16[64,1024]{1,0:T(8,128)(2,1)} async-done(((bf16[64,4096]{1,0:T(8,128)(2,1)}), bf16[64,1024]{1,0:T(8,128)(2,1)}) %reduce-scatter.6.cloned.1.call-update) | async-done | bytes 131088 | tf_op jit(solution)/shard_map/reduce_scatter | solution.py:162
  518.0 13.5 %all_gather.48 = bf16[64,4096]{1,0:T(8,128)(2,1)S(1)} all-gather(bf16[64,1024]{1,0:T(8,128)(2,1)S(1)} %fusion.65), channel_id=1, replica_groups=mesh['section'=2,'blk'=16,'mp'=4] {'mp'}, dimensions={1}, use_global_device_ids=true | all-gather | bytes 655360 | tf_op jit(solution)/shard_map/all_gather | solution.py:105
  532.5 6.1 fusion.128
  539.4 6.9 all-to-all-start.1
  546.6 24.3 %all_gather.49 = bf16[1024,1,128]{2,0,1:T(8,128)(2,1)S(1)} all-gather(bf16[64,1,128]{2,0,1:T(8,128)(2,1)S(1)} %pad_maximum_fusion.1), channel_id=1, replica_groups=mesh['section'=2,'blk'=16,'mp'=4] {'blk'}, dimensions={0}, use_global_device_ids=true | all-gather | bytes 278528 | tf_op jit(solution)/shard_map/all_gather | solution.py:127
  590.6 15.2 %reduce-scatter.8.cloned.1.call-done = bf16[64,1024]{1,0:T(8,128)(2,1)} async-done(((bf16[64,4096]{1,0:T(8,128)(2,1)}), bf16[64,1024]{1,0:T(8,128)(2,1)}) %reduce-scatter.8.cloned.1.call-update) | async-done | bytes 131088 | tf_op jit(solution)/shard_map/reduce_scatter | solution.py:162
  609.0 13.5 %all_gather.50 = bf16[64,4096]{1,0:T(8,128)(2,1)S(1)} all-gather(bf16[64,1024]{1,0:T(8,128)(2,1)S(1)} %broadcast_select_fusion.3), channel_id=1, replica_groups=mesh['section'=2,'blk'=16,'mp'=4] {'mp'}, dimensions={1}, use_global_device_ids=true | all-gather | bytes 655360 | tf_op jit(solution)/shard_map/all_gather | solution.py:105
  623.6 6.1 fusion.131
  630.5 6.8 all-to-all-start.2
  637.7 24.5 %all_gather.51 = bf16[1024,1,128]{2,0,1:T(8,128)(2,1)S(1)} all-gather(bf16[64,1,128]{2,0,1:T(8,128)(2,1)S(1)} %pad_maximum_fusion.2), channel_id=1, replica_groups=mesh['section'=2,'blk'=16,'mp'=4] {'blk'}, dimensions={0}, use_global_device_ids=true | all-gather | bytes 278528 | tf_op jit(solution)/shard_map/all_gather | solution.py:127
  676.9 5.7 fusion.19
  684.0 18.3 %reduce-scatter.10.cloned.1.call-done = bf16[64,1024]{1,0:T(8,128)(2,1)} async-done(((bf16[64,4096]{1,0:T(8,128)(2,1)}), bf16[64,1024]{1,0:T(8,128)(2,1)}) %reduce-scatter.10.cloned.1.call-update) | async-done | bytes 131088 | tf_op jit(solution)/shard_map/reduce_scatter | solution.py:162
  706.4 13.4 %all_gather.52 = bf16[64,4096]{1,0:T(8,128)(2,1)S(1)} all-gather(bf16[64,1024]{1,0:T(8,128)(2,1)S(1)} %broadcast_select_fusion.2), channel_id=1, replica_groups=mesh['section'=2,'blk'=16,'mp'=4] {'mp'}, dimensions={1}, use_global_device_ids=true | all-gather | bytes 655360 | tf_op jit(solution)/shard_map/all_gather | solution.py:105
  720.8 6.8 fusion.134
  728.4 6.9 all-to-all-start.3
  735.6 24.2 %all_gather.53 = bf16[1024,1,128]{2,0,1:T(8,128)(2,1)S(1)} all-gather(bf16[64,1,128]{2,0,1:T(8,128)(2,1)S(1)} %pad_maximum_fusion.3), channel_id=1, replica_groups=mesh['section'=2,'blk'=16,'mp'=4] {'blk'}, dimensions={0}, use_global_device_ids=true | all-gather | bytes 278528 | tf_op jit(solution)/shard_map/all_gather | solution.py:127
  772.0 5.0 fusion.76
  777.2 5.7 fusion.22
  783.0 19.5 %reduce-scatter.12.cloned.1.call-done = bf16[64,1024]{1,0:T(8,128)(2,1)} async-done(((bf16[64,4096]{1,0:T(8,128)(2,1)}), bf16[64,1024]{1,0:T(8,128)(2,1)}) %reduce-scatter.12.cloned.1.call-update) | async-done | bytes 131088 | tf_op jit(solution)/shard_map/reduce_scatter | solution.py:162
  811.2 12.8 %all_gather.54 = bf16[64,4096]{1,0:T(8,128)(2,1)S(1)} all-gather(bf16[64,1024]{1,0:T(8,128)(2,1)S(1)} %broadcast_select_fusion.1), channel_id=1, replica_groups=mesh['section'=2,'blk'=16,'mp'=4] {'mp'}, dimensions={1}, use_global_device_ids=true | all-gather | bytes 655360 | tf_op jit(solution)/shard_map/all_gather | solution.py:105
  825.0 6.1 fusion.137
  831.9 6.8 all-to-all-start.4
  839.1 24.3 %all_gather.55 = bf16[1024,1,128]{2,0,1:T(8,128)(2,1)S(1)} all-gather(bf16[64,1,128]{2,0,1:T(8,128)(2,1)S(1)} %pad_maximum_fusion.4), channel_id=1, replica_groups=mesh['section'=2,'blk'=16,'mp'=4] {'blk'}, dimensions={0}, use_global_device_ids=true | all-gather | bytes 278528 | tf_op jit(solution)/shard_map/all_gather | solution.py:127
  876.7 5.9 fusion.25
  883.4 18.7 %reduce-scatter.14.cloned.1.call-done = bf16[64,1024]{1,0:T(8,128)(2,1)} async-done(((bf16[64,4096]{1,0:T(8,128)(2,1)}), bf16[64,1024]{1,0:T(8,128)(2,1)}) %reduce-scatter.14.cloned.1.call-update) | async-done | bytes 131088 | tf_op jit(solution)/shard_map/reduce_scatter | solution.py:162
  (304 shorter events, 132.9 us)
Async XLA Ops:
  6.5 419.8 %all-gather.4.cloned.1.call-start = ((), (), s32[]{:S(2)}) async-start(), calls=%async_computation.10 | async-start | bytes 2228224 | tf_op jit(solution)/shard_map/all_gather | solution.py:74
  7.3 458.8 %all-gather.6.cloned.1.call-start = ((), (), s32[]{:S(2)}) async-start(), calls=%async_computation.11 | async-start | bytes 8912896 | tf_op jit(solution)/shard_map/all_gather | solution.py:73
  8.0 479.3 %all-gather.8.cloned.1.call-start = ((), (), s32[]{:S(2)}) async-start(), calls=%async_computation.12 | async-start | bytes 8912896 | tf_op jit(solution)/shard_map/all_gather | solution.py:75
  21.4 385.7 %copy-start.25 = (s32[256]{0:T(256)S(1)}, s32[256]{0:T(256)}, u32[]{:S(2)}) copy-start(s32[256]{0:T(256)} %param.18) | copy-start | bytes 3076
  21.4 403.5 %slice-start.2 = ((s32[4096]{0:T(1024)}), s32[1024]{0:T(1024)S(1)}, s32[]{:S(2)}) async-start(s32[4096]{0:T(1024)} %param.19), calls=%async_computation.20 | async-start | bytes 8192 | tf_op jit(solution)/shard_map/slice | solution.py:151
  21.4 404.9 %copy-start.46 = (f32[64]{0:T(128)}, f32[64]{0:T(128)S(1)}, u32[]{:S(2)}) copy-start(f32[64]{0:T(128)S(1)} %get-tuple-element.74) | copy-start | bytes 772
  22.2 524.1 %copy-start.26 = (f32[64]{0:T(128)}, f32[64]{0:T(128)S(1)}, u32[]{:S(2)}) copy-start(f32[64]{0:T(128)S(1)} %multiply_exponential_fusion) | copy-start | bytes 772
  22.2 384.8 %copy-start.44 = (s32[64]{0:T(128)}, s32[64]{0:T(128)S(1)}, u32[]{:S(2)}) copy-start(s32[64]{0:T(128)S(1)} %iota_add_fusion.5) | copy-start | bytes 772
  22.2 384.8 %copy-start.29 = (s32[64]{0:T(128)}, s32[64]{0:T(128)S(1)}, u32[]{:S(2)}) copy-start(s32[64]{0:T(128)S(1)} %get-tuple-element.77) | copy-start | bytes 772
  22.2 404.1 %copy-start.40 = (f32[64]{0:T(128)}, f32[64]{0:T(128)S(1)}, u32[]{:S(2)}) copy-start(f32[64]{0:T(128)S(1)} %get-tuple-element.80) | copy-start | bytes 772
  22.3 404.1 %copy-start.42 = (f32[64]{0:T(128)}, f32[64]{0:T(128)S(1)}, u32[]{:S(2)}) copy-start(f32[64]{0:T(128)S(1)} %get-tuple-element.79) | copy-start | bytes 772
  22.3 384.8 %copy-start.32 = (s32[64]{0:T(128)}, s32[64]{0:T(128)S(1)}, u32[]{:S(2)}) copy-start(s32[64]{0:T(128)S(1)} %get-tuple-element.75) | copy-start | bytes 772
  22.3 384.8 %copy-start.34 = (s32[64]{0:T(128)}, s32[64]{0:T(128)S(1)}, u32[]{:S(2)}) copy-start(s32[64]{0:T(128)S(1)} %get-tuple-element.76) | copy-start | bytes 772
  22.3 404.0 %copy-start.36 = (f32[64]{0:T(128)}, f32[64]{0:T(128)S(1)}, u32[]{:S(2)}) copy-start(f32[64]{0:T(128)S(1)} %get-tuple-element.82) | copy-start | bytes 772
  22.3 404.0 %copy-start.38 = (f32[64]{0:T(128)}, f32[64]{0:T(128)S(1)}, u32[]{:S(2)}) copy-start(f32[64]{0:T(128)S(1)} %get-tuple-element.81) | copy-start | bytes 772
  432.7 30.6 %all-to-all-start = ((bf16[16,64,1,128]{3,1,2,0:T(8,128)(2,1)}), bf16[16,64,1,128]{3,1,2,0:T(8,128)(2,1)}, u32[]{:S(2)}, u32[]{:S(2)}) async-start(bf16[16,64,1,128]{3,1,2,0:T(8,128)(2,1)} %stack.10), calls=%async_computation | async-start | bytes 524288 | tf_op jit(solution)/shard_map/all_to_all | solution.py:129
  436.9 75.8 %reduce-scatter.6.cloned.1.call-start = ((), (), s32[]{:S(2)}) async-start(), calls=%async_computation.13 | async-start | bytes 655360 | tf_op jit(solution)/shard_map/reduce_scatter | solution.py:162
  513.7 2.5 collective-permute-start
  532.5 40.1 %copy-start.22 = (f32[64,64]{1,0:T(8,128)S(1)}, f32[64,64]{1,0:T(8,128)}, u32[]{:S(2)}) copy-start(f32[64,64]{1,0:T(8,128)} %get-tuple-element.51) | copy-start | bytes 49156
  539.4 38.8 %all-to-all-start.1 = ((bf16[16,64,1,128]{3,1,2,0:T(8,128)(2,1)}), bf16[16,64,1,128]{3,1,2,0:T(8,128)(2,1)}, u32[]{:S(2)}, u32[]{:S(2)}) async-start(bf16[16,64,1,128]{3,1,2,0:T(8,128)(2,1)} %stack.11), calls=%async_computation.2 | async-start | bytes 524288 | tf_op jit(solution)/shard_map/all_to_all | solution.py:129
  546.3 59.5 %reduce-scatter.8.cloned.1.call-start = ((), (), s32[]{:S(2)}) async-start(), calls=%async_computation.14 | async-start | bytes 655360 | tf_op jit(solution)/shard_map/reduce_scatter | solution.py:162
  606.7 2.3 collective-permute-start.1
  623.6 40.2 %copy-start.21 = (f32[64,64]{1,0:T(8,128)S(1)}, f32[64,64]{1,0:T(8,128)}, u32[]{:S(2)}) copy-start(f32[64,64]{1,0:T(8,128)} %get-tuple-element.53) | copy-start | bytes 49156
  630.5 40.4 %all-to-all-start.2 = ((bf16[16,64,1,128]{3,1,2,0:T(8,128)(2,1)}), bf16[16,64,1,128]{3,1,2,0:T(8,128)(2,1)}, u32[]{:S(2)}, u32[]{:S(2)}) async-start(bf16[16,64,1,128]{3,1,2,0:T(8,128)(2,1)} %stack.12), calls=%async_computation.4 | async-start | bytes 524288 | tf_op jit(solution)/shard_map/all_to_all | solution.py:129
  637.3 64.9 %reduce-scatter.10.cloned.1.call-start = ((), (), s32[]{:S(2)}) async-start(), calls=%async_computation.15 | async-start | bytes 655360 | tf_op jit(solution)/shard_map/reduce_scatter | solution.py:162
  703.3 2.5 collective-permute-start.2
  720.8 40.7 %copy-start.20 = (f32[64,64]{1,0:T(8,128)S(1)}, f32[64,64]{1,0:T(8,128)}, u32[]{:S(2)}) copy-start(f32[64,64]{1,0:T(8,128)} %get-tuple-element.55) | copy-start | bytes 49156
  728.4 41.9 %all-to-all-start.3 = ((bf16[16,64,1,128]{3,1,2,0:T(8,128)(2,1)}), bf16[16,64,1,128]{3,1,2,0:T(8,128)(2,1)}, u32[]{:S(2)}, u32[]{:S(2)}) async-start(bf16[16,64,1,128]{3,1,2,0:T(8,128)(2,1)} %stack.13), calls=%async_computation.6 | async-start | bytes 524288 | tf_op jit(solution)/shard_map/all_to_all | solution.py:129
  735.2 67.2 %reduce-scatter.12.cloned.1.call-start = ((), (), s32[]{:S(2)}) async-start(), calls=%async_computation.16 | async-start | bytes 655360 | tf_op jit(solution)/shard_map/reduce_scatter | solution.py:162
  803.5 7.0 collective-permute-start.3
  831.9 38.9 %all-to-all-start.4 = ((bf16[16,64,1,128]{3,1,2,0:T(8,128)(2,1)}), bf16[16,64,1,128]{3,1,2,0:T(8,128)(2,1)S(1)}, u32[]{:S(2)}, u32[]{:S(2)}) async-start(bf16[16,64,1,128]{3,1,2,0:T(8,128)(2,1)} %stack.14), calls=%async_computation.8 | async-start | bytes 524288 | tf_op jit(solution)/shard_map/all_to_all | solution.py:129
  838.8 63.3 %reduce-scatter.14.cloned.1.call-start = ((), (), s32[]{:S(2)}) async-start(), calls=%async_computation.17 | async-start | bytes 655360 | tf_op jit(solution)/shard_map/reduce_scatter | solution.py:162
  (49 other events, 568.6 us)
Sparse Core Ops, SparseCore 0:
  9.5 47.7 all-gather.3
  59.5 74.0 all-gather.5
  135.7 81.6 all-gather.7
  493.3 19.3 reduce-scatter.5
  586.4 19.3 reduce-scatter.7
  682.8 19.3 reduce-scatter.9
  783.1 19.3 reduce-scatter.11
  882.7 19.3 reduce-scatter.13
